TPU v7x, 32 devices: a whole 2x2x4 slice. The times are simulated.
32 devices in a mesh: cores: 4 (over y, x), row: 4 (over z), tensor: 2 (over core).
Axes of the slice: x: 2, y: 2, z: 4, core: 2. Of those that a mesh axis runs over, the one named last changes fastest.
Arguments:
- cores: float32 [2, 4, 128, 256, 256], P('tensor', 'cores', 'row'), may hold values from -1 to 1, as said below
- incoming: float32 [2, 256, 256], P('tensor'), may hold values from -1 to 2, as said below
Outputs:
- frames: float32 [2, 4, 128, 256, 256], P('tensor', 'cores', 'row')
- tail: float32 [2, 256, 256], P('tensor', 'cores')
- correlation: float32 [2, 256, 256], P('tensor', 'cores')
Inputs may be any that keep to these rules, and one draw needn't show every extreme that they name: `cores`: each core's unfolding over (mode index, left rank) has full column rank and is well conditioned. `incoming`: upper triangular, diagonal entries from 1 to 2.
All inputs are finite; a program needn't handle non-finite values.
Results may differ from a plain program's by a relative error of at most 0.0001.
Values sent between devices are 32-bit elements; how exact they have to be, the bound alone decides.
A program may use at most 192 MiB of HBM per device.

v0:
```python
import jax
import jax.numpy as jnp
from jax import lax
from jax.sharding import PartitionSpec as P

RANK = 256
MODE = 128


HIGH_PRECISION = lax.Precision.HIGHEST


def swapped(value, axis, distance):
    mask = 2**distance
    pairs = [(source, source ^ mask) for source in range(lax.axis_size(axis))]
    return lax.ppermute(value, axis, pairs)


def passed_along(value, axis, steps):
    count = lax.axis_size(axis)
    first, last = (max(0, -steps), min(count, count - steps))
    return lax.ppermute(value, axis, [(source, source + steps) for source in range(first, last)])


def spread(value, axis, source):
    kept = jnp.where(lax.axis_index(axis) == source, value, 0).astype(value.dtype)
    return lax.psum(kept, axis)


def mix_block(upper, block):
    return jnp.einsum("ab,ibc->iac", upper, block, precision=HIGH_PRECISION)


def gram_of(mixed_gram):
    return jnp.einsum("bgk,bgj->kj", mixed_gram, mixed_gram, precision=HIGH_PRECISION)


def link_part(link, left, right):
    middle = jnp.einsum("bc,icd->ibd", link, right, precision=HIGH_PRECISION)
    return jnp.einsum("iba,ibd->ad", left, middle, precision=HIGH_PRECISION)


def make_frame(mixed_gram, gram_matrix):
    lower = jnp.linalg.cholesky(gram_matrix)
    identity_matrix = jnp.eye(gram_matrix.shape[0], dtype=gram_matrix.dtype)
    inverse_factor = lax.linalg.triangular_solve(lower, identity_matrix, left_side=True, lower=True)
    basis_frame = jnp.einsum("pwv,kv->pwk", mixed_gram, inverse_factor, precision=HIGH_PRECISION)
    return (basis_frame, lower.T)


def shards(cores, incoming):
    rank = cores.shape[-1]
    factor = float(MODE * RANK) ** 0.5
    section = lax.axis_index("cores")
    train_sections = lax.axis_size("cores")
    own = cores[0]
    upper_start = incoming[0]
    partner, partner_in = swapped((cores, incoming), "tensor", 0)
    partner_blocks = partner[0]
    link_start = jnp.dot(upper_start.T, partner_in[0], precision=HIGH_PRECISION)
    upper = upper_start
    link = link_start
    result = jnp.zeros_like(own)
    for tick in range(train_sections):
        if tick > 0:
            got_upper, got_link = passed_along((upper, link), "cores", 1)
            upper = jnp.where(section < tick, upper_start, got_upper)
            link = jnp.where(section < tick, link_start, got_link)
        active = section == tick
        block = own[0]
        other_block = partner_blocks[0]

        def busy_terms(operands):
            upper_now, link_now = operands
            mixed_now = mix_block(upper_now, block)
            return (mixed_now, gram_of(mixed_now), link_part(link_now, block, other_block))

        def quiet_terms(operands):
            upper_now, link_now = operands
            return (jnp.zeros_like(block), jnp.zeros_like(upper_now), jnp.zeros_like(link_now))

        mixed_gram, local_gram, partial_bond = lax.cond(
            active, busy_terms, quiet_terms, (upper, link)
        )

        def busy_frame(operands):
            mixed_now, gram_now, upper_now = operands
            return make_frame(mixed_now, gram_now)

        def quiet_frame(operands):
            mixed_now, gram_now, upper_now = operands
            return (jnp.zeros_like(mixed_now), upper_now)

        gram_matrix, summed_bond = lax.psum((local_gram, partial_bond), "row")
        basis_frame, upper = lax.cond(
            active, busy_frame, quiet_frame, (mixed_gram, gram_matrix, upper)
        )
        link = jnp.where(active, summed_bond, link)
        new_blocks = [basis_frame]
        stacked = jnp.stack(new_blocks)
        result = jnp.where(active, stacked, result)
    tail, link = (
        spread(upper, "cores", train_sections - 1),
        spread(link, "cores", train_sections - 1),
    )
    share = rank // train_sections
    tail_rows = lax.dynamic_slice_in_dim(tail, section * share, share, 0)
    correlation_rows = lax.dynamic_slice_in_dim(link, section * share, share, 0)
    return ((result * factor)[None], tail_rows[None], correlation_rows[None])


def solution(mesh):
    in_specs = (P("tensor", "cores", "row", None, None), P("tensor", None, None))
    out_specs = (
        P("tensor", "cores", "row", None, None),
        P("tensor", "cores", None),
        P("tensor", "cores", None),
    )
    return jax.shard_map(shards, mesh=mesh, in_specs=in_specs, out_specs=out_specs, check_vma=False)
```

profile of v0, /device:TPU:1, one launch (start us, length us, event | category | flops | bytes accessed | tf_op | source)
XLA Modules:
  0.0 818.5 jit_solution(5132032545365121814)
XLA Ops:
  7.8 13.2 %collective-permute-done.1 = f32[1,256,256]{2,1,0:T(8,128)S(1)} collective-permute-done((f32[1,256,256]{2,1,0:T(8,128)}, f32[1,256,256]{2,1,0:T(8,128)S(1)}, u32[]{:S(2)}, u32[]{:S(2)}) %collective-permute-start.1) | collective-permute-done | bytes 262176 | tf_op jit(solution)/shard_map/ppermute | solution.py:16
  22.6 53.6 %conditional.8 = (f32[32,256,256]{1,2,0:T(8,128)}, f32[256,256]{1,0:T(8,128)S(1)}, f32[256,256]{1,0:T(8,128)S(1)}) conditional(s32[]{:T(128)} %convert_element_type.34, () %tuple.74, (f32[32,256,256]{2,1,0:T(8,128)}, f32[256,256]{1,0:T(8,128)}, f32[32,256,256]{2,1,0:T(8,128)}, f32[256,256]{1,0:T(8,128)S(1)}) %tuple.240), branch_computations={%region_0.0_spmd, %region_1.0_spmd} | conditional | flops 25769803776 | bytes 85459016 | solution.py:82
  22.6 17.7 %convolution_bitcast_fusion = f32[32,256,256]{1,2,0:T(8,128)} fusion(f32[32,256,256]{2,1,0:T(8,128)} %get-tuple-element.54, f32[256,256]{1,0:T(8,128)} %get-tuple-element.55), kind=kOutput, calls=%fused_computation.2 | convolution fusion | flops 6442450944 | bytes 17039360 | tf_op jit(solution)/shard_map/cond/branch_1_fun/ab,ibc->iac/dot_general | solution.py:31
  40.3 10.7 %convolution_bitcast_fusion.1 = f32[256,256]{1,0:T(8,128)S(1)} fusion(f32[32,256,256]{1,2,0:T(8,128)} %convolution_bitcast_fusion), kind=kOutput, calls=%fused_computation.4 | convolution fusion | flops 6442450944 | bytes 8650752 | tf_op jit(solution)/shard_map/cond/branch_1_fun/bgk,bgj->kj/dot_general | solution.py:35
  51.0 17.2 %fusion.5 = f32[32,256,256]{2,1,0:T(8,128)S(1)} fusion(f32[32,256,256]{2,1,0:T(8,128)} %get-tuple-element.56, f32[256,256]{1,0:T(8,128)S(1)} %get-tuple-element.57), kind=kOutput, calls=%fused_computation.5 | convolution fusion | flops 6442450944 | bytes 17039360 | tf_op jit(solution)/shard_map/cond/branch_1_fun/bc,icd->ibd/dot_general | solution.py:39
  68.3 7.0 fusion.2
  77.1 38.1 %all-reduce.18.cloned.1.call-done = (f32[256,256]{0,1:T(8,128)}, f32[256,256]{1,0:T(8,128)}) async-done(((f32[256,256]{0,1:T(8,128)}, f32[256,256]{1,0:T(8,128)}), (f32[256,256]{0,1:T(8,128)}, f32[256,256]{1,0:T(8,128)})) %all-reduce.18.cloned.1.call-update) | async-done | bytes 524304 | tf_op jit(solution)/shard_map/psum | solution.py:94
  115.3 84.2 %conditional.9 = (f32[256,256]{0,1:T(8,128)S(1)}, f32[32,256,256]{2,1,0:T(8,128)}) conditional(s32[]{:T(128)} %convert_element_type.34, (f32[256,256]{1,0:T(8,128)}) %tuple.241, (f32[256,256]{0,1:T(8,128)}, f32[32,256,256]{1,2,0:T(8,128)}) %tuple.76), branch_computations={%region_3.0_spmd, %region_4.11_spmd} | conditional | flops 6644547584 | bytes 38668504 | solution.py:95
  117.4 11.7 %cholesky.214 = f32[128,128]{1,0:T(8,128)S(1)} custom-call(f32[128,128]{1,0:T(8,128)S(1)} %cholesky.346), custom_call_target="Cholesky" | custom-call | tf_op jit(solution)/shard_map/cond/branch_1_fun/jit(cholesky)/cholesky | solution.py:44
  129.1 9.8 %custom-call.17 = f32[1,128,128]{1,2,0:T(8,128)S(1)} custom-call(f32[1,128,128]{2,1,0:T(8,128)S(1)} %get-tuple-element.232), custom_call_target="InvertDiagBlocksLowerTriangular" | custom-call | tf_op jit(solution)/shard_map/cond/branch_1_fun/jit(cholesky)/cholesky | solution.py:44
  139.5 11.7 %cholesky.231 = f32[128,128]{1,0:T(8,128)S(1)} custom-call(f32[128,128]{1,0:T(8,128)S(1)} %convolution_subtract_fusion.1), custom_call_target="Cholesky" | custom-call | tf_op jit(solution)/shard_map/cond/branch_1_fun/jit(cholesky)/cholesky | solution.py:44
  157.7 19.7 %custom-call.18 = f32[2,128,128]{1,2,0:T(8,128)S(1)} custom-call(f32[2,128,128]{2,1,0:T(8,128)S(1)} %get-tuple-element.147), custom_call_target="InvertDiagBlocksLowerTriangular" | custom-call | tf_op jit(solution)/shard_map/cond/branch_1_fun/triangular_solve/custom-call.0 | solution.py:46
  178.3 11.7 %convolution_bitcast_fusion.8 = f32[32,256,256]{1,2,0:T(8,128)} fusion(f32[32,256,256]{1,2,0:T(8,128)} %get-tuple-element.164, f32[128,256]{1,0:T(8,128)S(1)} %fusion.42, f32[128,256]{1,0:T(8,128)S(1)} %fusion.39), kind=kOutput, calls=%fused_computation.34 | convolution fusion | flops 6442516480 | bytes 17039360 | tf_op jit(solution)/shard_map/cond/branch_1_fun/pwv,kv->pwk/dot_general | solution.py:47
  190.1 9.0 %copy.60 = f32[32,256,256]{2,1,0:T(8,128)} copy(f32[32,256,256]{1,2,0:T(8,128)} %convolution_bitcast_fusion.8) | data formatting | bytes 16777216 | tf_op jit(solution)/shard_map/cond | solution.py:95
  210.9 12.6 %conditional.10 = (f32[32,256,256]{1,2,0:T(8,128)}, f32[256,256]{1,0:T(8,128)S(1)}, f32[256,256]{1,0:T(8,128)S(1)}) conditional(s32[]{:T(128)} %convert_element_type.33, () %tuple.77, (f32[32,256,256]{2,1,0:T(8,128)}, f32[256,256]{1,0:T(8,128)S(1)}, f32[32,256,256]{2,1,0:T(8,128)}, f32[256,256]{1,0:T(8,128)S(1)}) %tuple.237), branch_computations={%region_10.13_spmd, %region_11.14_spmd} | conditional | flops 25769803776 | bytes 85459016 | solution.py:82
  224.4 79.4 %all-reduce.16.cloned.1.call-done = (f32[256,256]{0,1:T(8,128)}, f32[256,256]{1,0:T(8,128)}) async-done(((f32[256,256]{0,1:T(8,128)}, f32[256,256]{1,0:T(8,128)}), (f32[256,256]{0,1:T(8,128)}, f32[256,256]{1,0:T(8,128)})) %all-reduce.16.cloned.1.call-update) | async-done | bytes 524304 | tf_op jit(solution)/shard_map/psum | solution.py:94
  307.8 12.8 %conditional.11 = (f32[256,256]{0,1:T(8,128)S(1)}, f32[32,256,256]{2,1,0:T(8,128)}) conditional(s32[]{:T(128)} %convert_element_type.33, (f32[256,256]{1,0:T(8,128)S(1)}) %tuple.117, (f32[256,256]{0,1:T(8,128)}, f32[32,256,256]{1,2,0:T(8,128)}) %tuple.79), branch_computations={%region_13.16_spmd, %region_14.17_spmd} | conditional | flops 6644547584 | bytes 38668504 | solution.py:95
  320.8 73.5 %collective-permute-start.4 = (f32[256,256]{1,0:T(8,128)S(1)}, f32[256,256]{1,0:T(8,128)S(1)}, u32[]{:S(2)}, u32[]{:S(2)}) collective-permute-start(f32[256,256]{1,0:T(8,128)S(1)} %copy.29), channel_id=1, source_target_pairs={{0,8},{8,16},{16,24},{1,9},{9,17},{17,25},{2,10},{10,18},{18,26},{... | collective-permute-start | bytes 786440 | tf_op jit(solution)/shard_map/ppermute | solution.py:22
  398.1 12.8 %conditional.12 = (f32[32,256,256]{1,2,0:T(8,128)}, f32[256,256]{1,0:T(8,128)S(1)}, f32[256,256]{1,0:T(8,128)S(1)}) conditional(s32[]{:T(128)} %convert_element_type.32, () %tuple.80, (f32[32,256,256]{2,1,0:T(8,128)}, f32[256,256]{1,0:T(8,128)S(1)}, f32[32,256,256]{2,1,0:T(8,128)}, f32[256,256]{1,0:T(8,128)S(1)}) %tuple.238), branch_computations={%region_16.19_spmd, %region_17.20_spmd} | conditional | flops 25769803776 | bytes 85459016 | solution.py:82
  411.8 79.0 %all-reduce.14.cloned.1.call-done = (f32[256,256]{0,1:T(8,128)}, f32[256,256]{1,0:T(8,128)}) async-done(((f32[256,256]{0,1:T(8,128)}, f32[256,256]{1,0:T(8,128)}), (f32[256,256]{0,1:T(8,128)}, f32[256,256]{1,0:T(8,128)})) %all-reduce.14.cloned.1.call-update) | async-done | bytes 524304 | tf_op jit(solution)/shard_map/psum | solution.py:94
  494.0 12.8 %conditional.13 = (f32[256,256]{0,1:T(8,128)S(1)}, f32[32,256,256]{2,1,0:T(8,128)}) conditional(s32[]{:T(128)} %convert_element_type.32, (f32[256,256]{1,0:T(8,128)S(1)}) %tuple.122, (f32[256,256]{0,1:T(8,128)}, f32[32,256,256]{1,2,0:T(8,128)}) %tuple.82), branch_computations={%region_19.22_spmd, %region_20.23_spmd} | conditional | flops 6644547584 | bytes 38668504 | solution.py:95
  514.8 12.5 %conditional.14 = (f32[32,256,256]{1,2,0:T(8,128)}, f32[256,256]{1,0:T(8,128)S(1)}, f32[256,256]{1,0:T(8,128)S(1)}) conditional(s32[]{:T(128)} %convert_element_type.31, () %tuple.83, (f32[32,256,256]{2,1,0:T(8,128)}, f32[256,256]{1,0:T(8,128)S(1)}, f32[32,256,256]{2,1,0:T(8,128)}, f32[256,256]{1,0:T(8,128)S(1)}) %tuple.239), branch_computations={%region_22.25_spmd, %region_23.26_spmd} | conditional | flops 25769803776 | bytes 85459016 | solution.py:82
  528.2 149.9 %all-reduce.12.cloned.1.call-done = (f32[256,256]{0,1:T(8,128)}, f32[256,256]{1,0:T(8,128)}) async-done(((f32[256,256]{0,1:T(8,128)}, f32[256,256]{1,0:T(8,128)}), (f32[256,256]{0,1:T(8,128)}, f32[256,256]{1,0:T(8,128)})) %all-reduce.12.cloned.1.call-update) | async-done | bytes 524304 | tf_op jit(solution)/shard_map/psum | solution.py:94
  692.7 115.8 %all-reduce.20.cloned.1.call-done = (f32[256,256]{1,0:T(8,128)}, f32[256,256]{1,0:T(8,128)}) async-done(((f32[256,256]{1,0:T(8,128)}, f32[256,256]{1,0:T(8,128)}), (f32[256,256]{1,0:T(8,128)}, f32[256,256]{1,0:T(8,128)})) %all-reduce.20.cloned.1.call-update) | async-done | bytes 524304 | tf_op jit(solution)/shard_map/psum | solution.py:27
  (106 shorter events, 93.0 us)
Async XLA Ops:
  7.2 108.1 %all-reduce.18.cloned.1.call-start = ((), (), s32[]{:S(2)}) async-start(), calls=%async_computation.3 | async-start | bytes 1048576 | tf_op jit(solution)/shard_map/psum | solution.py:94
  7.2 15.4 %collective-permute-start = (f32[1,1,32,256,256]{4,3,2,1,0:T(8,128)}, f32[1,1,32,256,256]{4,3,2,1,0:T(8,128)}, u32[]{:S(2)}, u32[]{:S(2)}) collective-permute-start(f32[1,1,32,256,256]{4,3,2,1,0:T(8,128)} %param.21), channel_id=1, source_target_pairs={{0,1},{1,0},{2,3},{3,2},{4,5},{5,4},{6,7},{7,6},{8,9},{9,8},{10,11... | collective-permute-start | bytes 25165832 | tf_op jit(solution)/shard_map/ppermute | solution.py:16
  7.3 13.7 %collective-permute-start.1 = (f32[1,256,256]{2,1,0:T(8,128)}, f32[1,256,256]{2,1,0:T(8,128)S(1)}, u32[]{:S(2)}, u32[]{:S(2)}) collective-permute-start(f32[1,256,256]{2,1,0:T(8,128)} %param.22), channel_id=1, source_target_pairs={{0,1},{1,0},{2,3},{3,2},{4,5},{5,4},{6,7},{7,6},{8,9},{9,8},{10,11... | collective-permute-start | bytes 786440 | tf_op jit(solution)/shard_map/ppermute | solution.py:16
  40.3 28.0 %slice-start = ((s8[8388608]{0:T(1024)(128)(4,1)}), s8[4194304]{0:T(1024)(128)(4,1)S(1)}, s32[]{:S(2)}) async-start(s8[8388608]{0:T(1024)(128)(4,1)} %bitcast.273), calls=%async_computation.5 | async-start | bytes 8388608 | tf_op jit(solution)/shard_map/cond
  51.0 17.3 %slice-start.1 = ((s8[8388608]{0:T(1024)(128)(4,1)}), s8[4194304]{0:T(1024)(128)(4,1)S(1)}, s32[]{:S(2)}) async-start(s8[8388608]{0:T(1024)(128)(4,1)} %bitcast.273), calls=%async_computation.6 | async-start | bytes 8388608 | tf_op jit(solution)/shard_map/cond
  76.2 0.9 copy-start.1
  77.1 226.6 %all-reduce.16.cloned.1.call-start = ((), (), s32[]{:S(2)}) async-start(), calls=%async_computation.2 | async-start | bytes 1048576 | tf_op jit(solution)/shard_map/psum | solution.py:94
  115.3 85.6 %copy-start.6 = (f32[256,256]{1,0:T(8,128)S(1)}, f32[256,256]{1,0:T(8,128)}, u32[]{:S(2)}) copy-start(f32[256,256]{1,0:T(8,128)} %get-tuple-element.222) | copy-start | bytes 786436
  199.6 5.6 collective-permute-start.2
  200.9 9.9 %collective-permute-start.3 = (f32[256,256]{1,0:T(8,128)S(1)}, f32[256,256]{1,0:T(8,128)S(1)}, u32[]{:S(2)}, u32[]{:S(2)}) collective-permute-start(f32[256,256]{1,0:T(8,128)S(1)} %broadcast_select_fusion.3), channel_id=1, source_target_pairs={{0,8},{8,16},{16,24},{1,9},{9,17},{17,25},{2,10},{10,18},{18,26},{... | collective-permute-start | bytes 786440 | tf_op jit(solution)/shard_map/ppermute | solution.py:22
  223.4 0.9 copy-start.2
  224.3 266.5 %all-reduce.14.cloned.1.call-start = ((), (), s32[]{:S(2)}) async-start(), calls=%async_computation.1 | async-start | bytes 1048576 | tf_op jit(solution)/shard_map/psum | solution.py:94
  303.8 90.6 %collective-permute-start.5 = (f32[256,256]{1,0:T(8,128)S(1)}, f32[256,256]{1,0:T(8,128)S(1)}, u32[]{:S(2)}, u32[]{:S(2)}) collective-permute-start(f32[256,256]{1,0:T(8,128)S(1)} %broadcast_select_fusion.2), channel_id=1, source_target_pairs={{0,8},{8,16},{16,24},{1,9},{9,17},{17,25},{2,10},{10,18},{18,26},{... | collective-permute-start | bytes 786440 | tf_op jit(solution)/shard_map/ppermute | solution.py:22
  307.8 90.3 %copy-start = (f32[1,256,256]{2,1,0:T(8,128)S(1)}, f32[1,256,256]{2,1,0:T(8,128)}, u32[]{:S(2)}) copy-start(f32[1,256,256]{2,1,0:T(8,128)} %param.22) | copy-start | bytes 786436
  320.8 77.3 %collective-permute-start.4 = (f32[256,256]{1,0:T(8,128)S(1)}, f32[256,256]{1,0:T(8,128)S(1)}, u32[]{:S(2)}, u32[]{:S(2)}) collective-permute-start(f32[256,256]{1,0:T(8,128)S(1)} %copy.29), channel_id=1, source_target_pairs={{0,8},{8,16},{16,24},{1,9},{9,17},{17,25},{2,10},{10,18},{18,26},{... | collective-permute-start | bytes 786440 | tf_op jit(solution)/shard_map/ppermute | solution.py:22
  410.9 0.9 copy-start.3
  411.8 266.3 %all-reduce.12.cloned.1.call-start = ((), (), s32[]{:S(2)}) async-start(), calls=%async_computation | async-start | bytes 1048576 | tf_op jit(solution)/shard_map/psum | solution.py:94
  490.9 20.1 %collective-permute-start.7 = (f32[256,256]{1,0:T(8,128)S(1)}, f32[256,256]{1,0:T(8,128)S(1)}, u32[]{:S(2)}, u32[]{:S(2)}) collective-permute-start(f32[256,256]{1,0:T(8,128)S(1)} %broadcast_select_fusion.1), channel_id=1, source_target_pairs={{0,8},{8,16},{16,24},{1,9},{9,17},{17,25},{2,10},{10,18},{18,26},{... | collective-permute-start | bytes 786440 | tf_op jit(solution)/shard_map/ppermute | solution.py:22
  507.0 7.8 collective-permute-start.6
  527.3 0.8 copy-start.4
  528.2 280.3 %all-reduce.20.cloned.1.call-start = ((), (), s32[]{:S(2)}) async-start(), calls=%async_computation.4 | async-start | bytes 1048576 | tf_op jit(solution)/shard_map/psum | solution.py:27
  678.1 6.6 copy-start.5
Sparse Core Ops, SparseCore 0:
  77.2 38.0 all-reduce.17
  224.4 79.2 all-reduce.15
  411.9 78.9 all-reduce.13
  528.3 149.7 all-reduce.11
  685.8 122.7 all-reduce.19
where the time goes:
time: 829 us; the launch traced here: 819 us
  waiting for transfers between devices  491 us (59%)
  starting transfers between devices  88.1 us (11%)
  matrix products  67.3 us (8%)
  other arithmetic  63.9 us (8%)
  local copies, waits for them, and re-layouts  47.6 us (6%)
  loops' own time  46.5 us (6%)
  between operations  14.6 us (2%)
    psum x4, waiting for transfers between devices, shards(): gram_matrix, summed_bond = lax.psum((local_gram, partial_bond), 'row')  346 us
    psum x1, waiting for transfers between devices, spread(): return lax.psum(kept, axis)  116 us
    ppermute x6, starting transfers between devices, passed_along(): lax.ppermute(value, axis, [(source, source + steps) for source in range(f...  87.3 us
    another operation x6, other arithmetic, make_frame(): lower = jnp.linalg.cholesky(gram_matrix)  34 us
    another operation x13, local copies, waits for them, and re-layouts  27.1 us
    another operation x4, loops' own time, shards(): lax.cond(active, busy_terms, quiet_terms, (upper, link))  25.4 us
    another operation x4, loops' own time, shards(): lax.cond(active, busy_frame, quiet_frame, (mixed_gram, gram_matrix, upper))  20.8 us
    another operation x4, other arithmetic, make_frame(): lax.linalg.triangular_solve(lower, identity_matrix, left_side=True, lower...  19.7 us
  transfers between devices with their start and end apart: 13, of which 10 were waited for; matrix products, arithmetic and copies ran while one was open for 2% of the time, Pallas kernels for 0%

commit v1 on v0

v1 whole, which is shorter than its diff:
```python
import functools

import jax
import jax.numpy as jnp
from jax import lax
from jax.experimental import pallas as pl
from jax.experimental.pallas import tpu as pltpu
from jax.sharding import PartitionSpec as P

MESH = pl.DeviceIdType.MESH
F32 = jnp.float32
BF16 = jnp.bfloat16
NEWTON_STEPS = 7


def split(x):
    hi = x.astype(BF16)
    return hi, (x - hi.astype(F32)).astype(BF16)


def left3(hi, lo):
    return jnp.concatenate([hi, hi, lo], axis=1)


def right3(hi, lo):
    return jnp.concatenate([hi, lo, hi], axis=0)


def right3t(hi, lo):
    return jnp.concatenate([hi, lo, hi], axis=1)


def dot(a, b):
    return jnp.dot(a, b, preferred_element_type=F32)


def dot_nt(a, b):
    return lax.dot_general(a, b, (((1,), (1,)), ((), ())), preferred_element_type=F32)


def mm(a, b):
    return dot(left3(*split(a)), right3(*split(b)))


def mm_nt(a, b):
    return dot_nt(left3(*split(a)), right3t(*split(b)))


def chain_kernel(
    S, R, group,
    cores_ref, incoming_ref,
    gin_out, gout_out, gfin_out, lfin_out,
    raw, other, in_other, c_hi, c_lo, ct_hi, ct_lo, o_hi, o_lo,
    gin, gout, gfin, lin, lfin, p_ref, q_ref, rs_p, rs_q, red_p, red_q, acc,
    raw_sem, pair_send, pair_recv,
    rsp_send, rsp_recv, rsq_send, rsq_recv,
    hop_send, hop_recv, lhop_send, lhop_recv,
    fout_send, fout_recv, ffin_send, ffin_recv, flin_send, flin_recv,
    gf_send, gf_recv, lf_send, lf_recv,
):
    s = lax.axis_index("cores")
    r = lax.axis_index("row")
    t = lax.axis_index("tensor")
    modes, n, _ = raw.shape
    half = modes // 2
    ch = n // R
    wide = n // 2

    def row_at(d):
        return lax.rem(r + d, R)

    def tens(e):
        return lax.rem(t + e, 2)

    def rows(k):
        return pl.ds(pl.multiple_of(k * ch, ch), ch)

    def cols(k):
        return pl.ds(pl.multiple_of(k * wide, wide), wide)

    barrier = pltpu.get_barrier_semaphore()
    greeted = 0
    for d in range(R):
        for e in range(2):
            for q in range(S):
                if d == 0 and e == 0 and q == 0:
                    continue
                if q > 0 and e > 0 and q != 1 and q != S - 1:
                    continue
                pl.semaphore_signal(
                    barrier, inc=1, device_id=(lax.rem(s + q, S), row_at(d), tens(e)), device_id_type=MESH
                )
                greeted += 1
    pl.semaphore_wait(barrier, greeted)

    def remote(src, dst, send, recv, to):
        return pltpu.make_async_remote_copy(
            src_ref=src, dst_ref=dst, send_sem=send, recv_sem=recv, device_id=to, device_id_type=MESH
        )

    partner = (s, r, tens(1))
    give = remote(cores_ref.at[pl.ds((1 - t) * half, half)], other, pair_send.at[0], pair_recv.at[0], partner)
    give_in = remote(incoming_ref, in_other, pair_send.at[1], pair_recv.at[1], partner)
    give_in.start()
    give.start()

    groups = modes // group
    loads = [
        pltpu.make_async_copy(cores_ref.at[pl.ds(k * group, group)], raw.at[pl.ds(k * group, group)], raw_sem.at[k])
        for k in range(groups)
    ]
    for load in loads:
        load.start()
    for k in range(groups):
        loads[k].wait()

        def prep(j, carry, k=k):
            i = k * group + j
            x = raw[i]
            hi, lo = split(x)
            c_hi[i] = hi
            c_lo[i] = lo
            thi, tlo = split(x.T)
            ct_hi[i] = thi
            ct_lo[i] = tlo
            return carry

        lax.fori_loop(0, group, prep, 0)

    def prep_other():
        give.wait()
        give_in.wait()

        def body(j, carry):
            hi, lo = split(other[j])
            o_hi[j] = hi
            o_lo[j] = lo
            return carry

        lax.fori_loop(0, half, body, 0)

    nxt = lax.rem(s + 1, S)

    def g_hop(d):
        return remote(red_p, gin.at[rows(r)], hop_send.at[d], hop_recv.at[d], (nxt, row_at(d), t))

    def l_hop(d, e):
        return remote(
            red_q, lin.at[rows(r), cols(t)], lhop_send.at[d, e], lhop_recv.at[d, e], (nxt, row_at(d), tens(e))
        )

    pairs = [(d, e) for d in range(R) for e in range(2)]
    others = pairs[1:]

    @pl.when(s == 0)
    def _():
        u = incoming_ref[...]
        gin[...] = mm(u.T, u)

    @pl.when(s > 0)
    def _():
        prep_other()
        for d in range(R):
            g_hop(d).wait_recv()

    def run(w_ref, hi_ref, lo_ref, first, count, transpose):
        w = w_ref[...]
        w3 = left3(*split(w.T if transpose else w))
        acc[...] = jnp.zeros_like(acc)

        def body(k, carry):
            lhs = []
            rhs = []
            for j in range(group):
                i = k * group + j
                y = dot(w3, right3(hi_ref[i], lo_ref[i]))
                rhs.append(right3(*split(y)))
                lhs.append(left3(ct_hi[first + i], ct_lo[first + i]))
            acc[...] += dot(jnp.concatenate(lhs, axis=1), jnp.concatenate(rhs, axis=0))
            return carry

        lax.fori_loop(0, count // group, body, 0)

    run(gin, c_hi, c_lo, 0, modes, False)
    p_ref[...] = acc[...]

    def rsp(d):
        return remote(p_ref.at[rows(row_at(d))], rs_p.at[d], rsp_send.at[d], rsp_recv.at[d], (s, row_at(d), t))

    for d in range(1, R):
        rsp(d).start()

    @pl.when(s == 0)
    def _():
        prep_other()
        u = incoming_ref[...]
        v = in_other[...]

        @pl.when(t == 0)
        def _():
            lin[...] = mm(u.T, v)

        @pl.when(t == 1)
        def _():
            lin[...] = mm(v.T, u)

    @pl.when(s > 0)
    def _():
        for d, e in pairs:
            l_hop(d, e).wait_recv()

    first = t * half

    @pl.when(t == 0)
    def _():
        run(lin, o_hi, o_lo, first, half, False)
        q_ref[...] = acc[...]

    @pl.when(t == 1)
    def _():
        run(lin, o_hi, o_lo, first, half, True)
        q_ref[...] = acc[...].T

    for d in range(1, R):
        rsp(d).wait_recv()
    total = p_ref[rows(r), :]
    for d in range(1, R):
        total += rs_p[d]
    red_p[...] = total
    gout[rows(r), :] = total

    def g_fin(q):
        return remote(red_p, gfin.at[rows(r)], gf_send.at[q], gf_recv.at[0], (lax.rem(s + q, S), r, t))

    @pl.when(s < S - 1)
    def _():
        for d in range(R):
            g_hop(d).start()

    @pl.when(s == S - 1)
    def _():
        gfin[rows(r), :] = red_p[...]
        for q in range(1, S):
            g_fin(q).start()

    def rsq(d, e):
        return remote(
            q_ref.at[rows(row_at(d)), cols(tens(e))], rs_q.at[d, e], rsq_send.at[d, e], rsq_recv.at[d, e],
            (s, row_at(d), tens(e)),
        )

    for d, e in others:
        rsq(d, e).start()
    for d, e in others:
        rsq(d, e).wait_recv()
    total = q_ref[rows(r), cols(t)]
    for d, e in others:
        total += rs_q[d, e]
    red_q[...] = total

    def l_fin(q):
        return remote(red_q, lfin.at[rows(r), cols(t)], lf_send.at[q], lf_recv.at[0], (lax.rem(s + q, S), r, t))

    @pl.when(s < S - 1)
    def _():
        for d, e in pairs:
            l_hop(d, e).start()

    @pl.when(s == S - 1)
    def _():
        lfin[rows(r), cols(t)] = red_q[...]
        for q in range(1, S):
            l_fin(q).start()

    def fan(buf, send, recv, d):
        return remote(buf.at[rows(r)], buf.at[rows(r)], send.at[d], recv.at[d], (s, row_at(d), t))

    def fan_l(d, e):
        return remote(
            lfin.at[rows(r), cols(t)], lfin.at[rows(r), cols(t)], flin_send.at[d, e], flin_recv.at[d, e],
            (s, row_at(d), tens(e)),
        )

    for d in range(1, R):
        fan(gout, fout_send, fout_recv, d).start()

    @pl.when(s < S - 1)
    def _():
        g_fin(0).wait_recv()

    for d in range(1, R):
        fan(gfin, ffin_send, ffin_recv, d).start()

    @pl.when(s < S - 1)
    def _():
        l_fin(0).wait_recv()

    for d, e in others:
        fan_l(d, e).start()

    for d in range(1, R):
        fan(gout, fout_send, fout_recv, d).wait_recv()
        fan(gfin, ffin_send, ffin_recv, d).wait_recv()
    for d, e in others:
        fan_l(d, e).wait_recv()
    gin_out[...] = gin[...]
    gout_out[...] = gout[...]
    gfin_out[...] = gfin[...]
    lfin_out[...] = lfin[...]
    for d in range(1, R):
        rsp(d).wait_send()
        fan(gout, fout_send, fout_recv, d).wait_send()
        fan(gfin, ffin_send, ffin_recv, d).wait_send()
    for d, e in others:
        rsq(d, e).wait_send()
        fan_l(d, e).wait_send()

    @pl.when(s < S - 1)
    def _():
        for d in range(R):
            g_hop(d).wait_send()
        for d, e in pairs:
            l_hop(d, e).wait_send()

    @pl.when(s == S - 1)
    def _():
        for q in range(1, S):
            g_fin(q).wait_send()
            l_fin(q).wait_send()


def chain(block, incoming, S, R):
    modes, n, _ = block.shape
    half = modes // 2
    group = 1
    while group < 4 and half % (2 * group) == 0:
        group *= 2
    ch = n // R
    dma = pltpu.SemaphoreType.DMA
    vmem = pltpu.VMEM
    full = jax.ShapeDtypeStruct((n, n), F32)
    return pl.pallas_call(
        functools.partial(chain_kernel, S, R, group),
        out_shape=[full] * 4,
        in_specs=[pl.BlockSpec(memory_space=pl.ANY), pl.BlockSpec(memory_space=pltpu.VMEM)],
        out_specs=[pl.BlockSpec(memory_space=pltpu.VMEM)] * 4,
        scratch_shapes=[
            vmem((modes, n, n), F32), vmem((half, n, n), F32), vmem((n, n), F32),
            vmem((modes, n, n), BF16), vmem((modes, n, n), BF16),
            vmem((modes, n, n), BF16), vmem((modes, n, n), BF16),
            vmem((half, n, n), BF16), vmem((half, n, n), BF16),
            vmem((n, n), F32), vmem((n, n), F32), vmem((n, n), F32), vmem((n, n), F32), vmem((n, n), F32),
            vmem((n, n), F32), vmem((n, n), F32),
            vmem((R, ch, n), F32), vmem((R, 2, ch, n // 2), F32),
            vmem((ch, n), F32), vmem((ch, n // 2), F32), vmem((n, n), F32),
            dma((modes // group,)), dma((2,)), dma((2,)),
            dma((R,)), dma((R,)), dma((R, 2)), dma((R, 2)),
            dma((R,)), dma((R,)), dma((R, 2)), dma((R, 2)),
            dma((R,)), dma((R,)), dma((R,)), dma((R,)), dma((R, 2)), dma((R, 2)),
            dma((S,)), dma((1,)), dma((S,)), dma((1,)),
        ],
        compiler_params=pltpu.CompilerParams(
            collective_id=0, has_side_effects=True, vmem_limit_bytes=60 * 1024 * 1024
        ),
        name="gram_chain",
    )(block, incoming)


def lower_part(e):
    row = lax.broadcasted_iota(jnp.int32, e.shape, 0)
    col = lax.broadcasted_iota(jnp.int32, e.shape, 1)
    return jnp.where(row > col, e, jnp.where(row == col, 0.5 * e, 0.0))


def frame_kernel(
    group, scale, g_ref, incoming_ref, blocks_ref, frames_ref, tail_ref, x_ref, a_ref, b_ref, u_hi, u_lo, x_hi, x_lo
):
    n = incoming_ref.shape[0]
    count = g_ref.shape[0]
    section = lax.axis_index("cores")
    sections = lax.axis_size("cores")

    @pl.when(pl.program_id(0) == 0)
    def _():
        row = lax.broadcasted_iota(jnp.int32, (n, n), 0)
        col = lax.broadcasted_iota(jnp.int32, (n, n), 1)
        eye = (row == col).astype(F32)
        for m in range(count):
            diagonal = jnp.sum(g_ref[m] * eye, axis=0, keepdims=True)
            x_ref[m] = eye * lax.rsqrt(diagonal)

        def residual(m):
            x = x_ref[m]
            return x, mm_nt(mm(x, g_ref[m]), x) - eye

        def step(k, carry):
            for m in range(count):
                x, e = residual(m)
                x_ref[m] = x - mm(lower_part(e), x)
            return carry

        lax.fori_loop(0, NEWTON_STEPS, step, 0)

        for m in range(count):
            x, e = residual(m)
            distance = jnp.sum(e * e)
            smallest = jnp.min(jnp.where(row == col, x, 1.0))

            @pl.when(jnp.logical_not((distance < 1e-6) & (smallest > 0.0)))
            def _(m=m):
                a_ref[...] = g_ref[m]
                b_ref[...] = eye

                def column(j, carry):
                    a = a_ref[...]
                    b = b_ref[...]
                    rowj = jnp.sum(jnp.where(row == j, a, 0.0), axis=0, keepdims=True)
                    pivot = jnp.sum(jnp.where((row == j) & (col == j), a, 0.0), keepdims=True)
                    inv = lax.rsqrt(pivot)
                    colj = jnp.sum(jnp.where(col == j, a, 0.0), axis=1, keepdims=True) * inv
                    below = lax.broadcasted_iota(jnp.int32, (n, 1), 0) > j
                    colj = jnp.where(below, colj, 0.0)
                    bj = jnp.sum(jnp.where(row == j, b, 0.0), axis=0, keepdims=True) * inv
                    a_ref[...] = a - colj * (rowj * inv)
                    b_ref[...] = jnp.where(row == j, bj, b) - colj * bj
                    return carry

                lax.fori_loop(0, n, column, 0)
                x_ref[m] = b_ref[...]

        def factor(m):
            return jnp.where(row <= col, mm(x_ref[m], g_ref[m]), 0.0)

        tail_ref[...] = factor(2)
        upper = jnp.where(section == 0, incoming_ref[...], factor(0))
        hi, lo = split(upper)
        u_hi[...] = hi
        u_lo[...] = lo
        hi, lo = split(jnp.where(row >= col, x_ref[1], 0.0).T * scale)
        x_hi[...] = hi
        x_lo[...] = lo

    u3 = left3(u_hi[...], u_lo[...])
    x3 = right3(x_hi[...], x_lo[...])
    for j in range(group):
        mixed = dot(u3, right3(*split(blocks_ref[j])))
        frames_ref[j] = dot(left3(*split(mixed)), x3)


def make_frames(grams, incoming, block, scale):
    modes, n, _ = block.shape
    group = min(4, modes)
    vmem = pltpu.VMEM
    return pl.pallas_call(
        functools.partial(frame_kernel, group, scale),
        grid=(modes // group,),
        out_shape=[jax.ShapeDtypeStruct((modes, n, n), F32), jax.ShapeDtypeStruct((n, n), F32)],
        in_specs=[
            pl.BlockSpec((3, n, n), lambda i: (0, 0, 0)),
            pl.BlockSpec((n, n), lambda i: (0, 0)),
            pl.BlockSpec((group, n, n), lambda i: (i, 0, 0)),
        ],
        out_specs=[
            pl.BlockSpec((group, n, n), lambda i: (i, 0, 0)),
            pl.BlockSpec((n, n), lambda i: (0, 0)),
        ],
        scratch_shapes=[
            vmem((3, n, n), F32), vmem((n, n), F32), vmem((n, n), F32),
            vmem((n, n), BF16), vmem((n, n), BF16), vmem((n, n), BF16), vmem((n, n), BF16),
        ],
        compiler_params=pltpu.CompilerParams(vmem_limit_bytes=48 * 1024 * 1024),
        name="frames",
    )(grams, incoming, block)


def shards(S, R, T, modes_all, cores, incoming):
    block = cores[0, 0]
    upper_start = incoming[0]
    n = block.shape[-1]
    section = lax.axis_index("cores")
    tensor = lax.axis_index("tensor")
    gin, gout, gfin, link = chain(block, upper_start, S, R)
    gin = jnp.where(section == 0, jnp.eye(n, dtype=F32), gin)
    gout = jnp.where(section == S - 1, gfin, gout)
    scale = float(modes_all * n) ** 0.5
    frames, tail = make_frames(jnp.stack([gin, gout, gfin]), upper_start, block, scale)
    share = n // S
    link = jnp.where(tensor == 0, link, link.T)
    tail_rows = lax.dynamic_slice_in_dim(tail, section * share, share, 0)
    link_rows = lax.dynamic_slice_in_dim(link, section * share, share, 0)
    return frames[None, None], tail_rows[None], link_rows[None]


def solution(mesh):
    S, R, T = (mesh.shape[name] for name in ("cores", "row", "tensor"))
    in_specs = (P("tensor", "cores", "row", None, None), P("tensor", None, None))
    out_specs = (
        P("tensor", "cores", "row", None, None),
        P("tensor", "cores", None),
        P("tensor", "cores", None),
    )

    def whole(cores, incoming):
        body = functools.partial(shards, S, R, T, cores.shape[2])
        return jax.shard_map(body, mesh=mesh, in_specs=in_specs, out_specs=out_specs, check_vma=False)(
            cores, incoming
        )

    return whole
```

time: 829 us -> 172 us (0.21)
  the two profiles are of different devices: /device:TPU:1 before, /device:TPU:31 now
where the time goes in v1:
time: 172 us
  Pallas kernels  166 us (97%)
  other arithmetic  3.58 us (2%)
  local copies, waits for them, and re-layouts  1.72 us (1%)
    pallas_call x1, Pallas kernels, chain(): pl.pallas_call(functools.partial(chain_kernel, S, R, group), out_shape=[f...  137 us
    pallas_call x1, Pallas kernels, make_frames(): pl.pallas_call(functools.partial(frame_kernel, group, scale), grid=(modes...  29.3 us

profile of v1, /device:TPU:31, one launch (start us, length us, event | category | flops | bytes accessed | tf_op | source)
XLA Modules:
  0.0 172.0 jit_solution(896570283925815163)
XLA Ops:
  0.6 0.0 copy-start
  0.7 136.7 %gram_chain.1 = (f32[256,256]{1,0:T(8,128)}, f32[256,256]{1,0:T(8,128)}, f32[256,256]{1,0:T(8,128)}, f32[256,256]{1,0:T(8,128)}) custom-call(f32[32,256,256]{2,1,0:T(8,128)} %bitcast.15, f32[256,256]{1,0:T(8,128)} %bitcast.13), custom_call_target="tpu_custom_call" | custom-call | tf_op jit(solution)/shard_map/gram_chain/pallas_call | solution.py:342
  137.4 1.1 select_bitcast_fusion
  138.5 1.0 pad_maximum_fusion.g_ref
  139.5 1.1 copy.5
  140.6 1.5 fusion
  142.1 0.0 copy-done
  142.1 29.3 %frames.1 = (f32[32,256,256]{2,1,0:T(8,128)}, f32[256,256]{1,0:T(8,128)S(1)}) custom-call(f32[3,256,256]{2,1,0:T(8,128)S(1)} %pad_maximum_fusion.g_ref, f32[256,256]{1,0:T(8,128)S(1)} %bitcast.14, f32[32,256,256]{2,1,0:T(8,128)} %bitcast.16), custom_call_target="tpu_custom_call" | custom-call | tf_op jit(solution)/shard_map/frames/pallas_call | solution.py:454
  171.3 0.6 dynamic-slice_bitcast_fusion
Async XLA Ops:
  0.6 141.4 %copy-start = (f32[1,256,256]{2,1,0:T(8,128)S(1)}, f32[1,256,256]{2,1,0:T(8,128)}, u32[]{:S(2)}) copy-start(f32[1,256,256]{2,1,0:T(8,128)} %param.3) | copy-start | bytes 786436

commit v2 on v1

--- a/solution.py
+++ b/solution.py
@@ -10,7 +10,8 @@
 MESH = pl.DeviceIdType.MESH
 F32 = jnp.float32
 BF16 = jnp.bfloat16
-NEWTON_STEPS = 7
+NEWTON_STEPS = 16
+CLOSE = 1e-6
 
 
 def split(x):
@@ -46,14 +47,30 @@
     return dot_nt(left3(*split(a)), right3t(*split(b)))
 
 
+def pack(g, blocks):
+    h = g.shape[0] // 2
+    parts = [g[:h, :h], g[:h, h:], g[h:, h:]]
+    if blocks == 4:
+        parts.append(g[h:, :h])
+    return jnp.concatenate(parts, axis=0)
+
+
+def unpack(p):
+    h = p.shape[1]
+    a, b, c = p[:h], p[h : 2 * h], p[2 * h : 3 * h]
+    return jnp.concatenate(
+        [jnp.concatenate([a, b], axis=1), jnp.concatenate([b.T, c], axis=1)], axis=0
+    )
+
+
 def chain_kernel(
-    S, R, group,
+    S, R, group, blocks,
     cores_ref, incoming_ref,
-    gin_out, gout_out, gfin_out, lfin_out,
+    grams_out, link_out,
     raw, other, in_other, c_hi, c_lo, ct_hi, ct_lo, o_hi, o_lo,
-    gin, gout, gfin, lin, lfin, p_ref, q_ref, rs_p, rs_q, red_p, red_q, acc,
+    gin, gout, gfin, lin, lfin, p_ref, q_ref, q_got, q_sum, rs_p, rs_q, red_p, red_q, acc, turned,
     raw_sem, pair_send, pair_recv,
-    rsp_send, rsp_recv, rsq_send, rsq_recv,
+    rsp_send, rsp_recv, rsq_send, rsq_recv, swap_send, swap_recv, half_send, half_recv,
     hop_send, hop_recv, lhop_send, lhop_recv,
     fout_send, fout_recv, ffin_send, ffin_recv, flin_send, flin_recv,
     gf_send, gf_recv, lf_send, lf_recv,
@@ -72,8 +89,13 @@
     def tens(e):
         return lax.rem(t + e, 2)
 
+    part = blocks * wide // R
+
     def rows(k):
         return pl.ds(pl.multiple_of(k * ch, ch), ch)
+
+    def parts(k):
+        return pl.ds(pl.multiple_of(k * part, part), part)
 
     def cols(k):
         return pl.ds(pl.multiple_of(k * wide, wide), wide)
@@ -85,7 +107,7 @@
             for q in range(S):
                 if d == 0 and e == 0 and q == 0:
                     continue
-                if q > 0 and e > 0 and q != 1 and q != S - 1:
+                if q > 0 and e > 0:
                     continue
                 pl.semaphore_signal(
                     barrier, inc=1, device_id=(lax.rem(s + q, S), row_at(d), tens(e)), device_id_type=MESH
@@ -142,12 +164,13 @@
     nxt = lax.rem(s + 1, S)
 
     def g_hop(d):
-        return remote(red_p, gin.at[rows(r)], hop_send.at[d], hop_recv.at[d], (nxt, row_at(d), t))
-
-    def l_hop(d, e):
-        return remote(
-            red_q, lin.at[rows(r), cols(t)], lhop_send.at[d, e], lhop_recv.at[d, e], (nxt, row_at(d), tens(e))
-        )
+        return remote(red_p, gin.at[parts(r)], hop_send.at[d], hop_recv.at[d], (nxt, row_at(d), t))
+
+    def l_hop(d):
+        return remote(red_q, lin.at[t, rows(r)], lhop_send.at[d], lhop_recv.at[d], (nxt, row_at(d), t))
+
+    def l_half():
+        return remote(lin.at[t], lin.at[t], half_send, half_recv, partner)
 
     pairs = [(d, e) for d in range(R) for e in range(2)]
     others = pairs[1:]
@@ -155,7 +178,7 @@
     @pl.when(s == 0)
     def _():
         u = incoming_ref[...]
-        gin[...] = mm(u.T, u)
+        gin[...] = pack(mm(u.T, u), blocks)
 
     @pl.when(s > 0)
     def _():
@@ -163,9 +186,8 @@
         for d in range(R):
             g_hop(d).wait_recv()
 
-    def run(w_ref, hi_ref, lo_ref, first, count, transpose):
-        w = w_ref[...]
-        w3 = left3(*split(w.T if transpose else w))
+    def run(w, hi_ref, lo_ref, first, count):
+        w3 = left3(*split(w))
         acc[...] = jnp.zeros_like(acc)
 
         def body(k, carry):
@@ -181,14 +203,18 @@
 
         lax.fori_loop(0, count // group, body, 0)
 
-    run(gin, c_hi, c_lo, 0, modes, False)
-    p_ref[...] = acc[...]
+    run(unpack(gin[...]), c_hi, c_lo, 0, modes)
+    p_ref[...] = pack(acc[...], blocks)
 
     def rsp(d):
-        return remote(p_ref.at[rows(row_at(d))], rs_p.at[d], rsp_send.at[d], rsp_recv.at[d], (s, row_at(d), t))
+        return remote(p_ref.at[parts(row_at(d))], rs_p.at[d], rsp_send.at[d], rsp_recv.at[d], (s, row_at(d), t))
 
     for d in range(1, R):
         rsp(d).start()
+
+    def put(m):
+        lin[0] = m[:, :wide]
+        lin[1] = m[:, wide:]
 
     @pl.when(s == 0)
     def _():
@@ -198,39 +224,53 @@
 
         @pl.when(t == 0)
         def _():
-            lin[...] = mm(u.T, v)
+            put(mm(u.T, v))
 
         @pl.when(t == 1)
         def _():
-            lin[...] = mm(v.T, u)
+            put(mm(v.T, u))
 
     @pl.when(s > 0)
     def _():
-        for d, e in pairs:
-            l_hop(d, e).wait_recv()
+        for d in range(R):
+            l_hop(d).wait_recv()
+        l_half().start()
+        l_half().wait_recv()
 
     first = t * half
+    link = jnp.concatenate([lin[0], lin[1]], axis=1)
 
     @pl.when(t == 0)
     def _():
-        run(lin, o_hi, o_lo, first, half, False)
-        q_ref[...] = acc[...]
+        run(link, o_hi, o_lo, first, half)
+        q_ref[0] = acc[:, :wide]
+        q_ref[1] = acc[:, wide:]
 
     @pl.when(t == 1)
     def _():
-        run(lin, o_hi, o_lo, first, half, True)
-        q_ref[...] = acc[...].T
+        run(link.T, o_hi, o_lo, first, half)
+        turned[...] = acc[...].T
+        q_ref[0] = turned[:, :wide]
+        q_ref[1] = turned[:, wide:]
+
+    swap = remote(q_ref.at[1 - t], q_got, swap_send, swap_recv, partner)
+    swap.start()
 
     for d in range(1, R):
         rsp(d).wait_recv()
-    total = p_ref[rows(r), :]
+    total = p_ref[parts(r), :]
     for d in range(1, R):
         total += rs_p[d]
     red_p[...] = total
-    gout[rows(r), :] = total
 
     def g_fin(q):
-        return remote(red_p, gfin.at[rows(r)], gf_send.at[q], gf_recv.at[0], (lax.rem(s + q, S), r, t))
+        return remote(red_p, gfin.at[parts(r)], gf_send.at[q], gf_recv.at[0], (lax.rem(s + q, S), r, t))
+
+    def fan(buf, send, recv, d):
+        return remote(red_p, buf.at[parts(r)], send.at[d], recv.at[d], (s, row_at(d), t))
+
+    def fan_fin(d):
+        return remote(gfin.at[parts(r)], gfin.at[parts(r)], ffin_send.at[d], ffin_recv.at[d], (s, row_at(d), t))
 
     @pl.when(s < S - 1)
     def _():
@@ -239,88 +279,114 @@
 
     @pl.when(s == S - 1)
     def _():
-        gfin[rows(r), :] = red_p[...]
+        gfin[parts(r), :] = red_p[...]
+        for d in range(1, R):
+            fan_fin(d).start()
         for q in range(1, S):
             g_fin(q).start()
 
-    def rsq(d, e):
+    swap.wait_recv()
+    q_sum[...] = q_ref[t] + q_got[...]
+
+    def rsq(d):
+        return remote(q_sum.at[rows(row_at(d))], rs_q.at[d], rsq_send.at[d], rsq_recv.at[d], (s, row_at(d), t))
+
+    for d in range(1, R):
+        rsq(d).start()
+    for d in range(1, R):
+        rsq(d).wait_recv()
+    total = q_sum[rows(r), :]
+    for d in range(1, R):
+        total += rs_q[d]
+    red_q[...] = total
+
+    def l_fin(q):
+        return remote(red_q, lfin.at[t, rows(r)], lf_send.at[q], lf_recv.at[0], (lax.rem(s + q, S), r, t))
+
+    def fan_l(d, e):
         return remote(
-            q_ref.at[rows(row_at(d)), cols(tens(e))], rs_q.at[d, e], rsq_send.at[d, e], rsq_recv.at[d, e],
-            (s, row_at(d), tens(e)),
+            lfin.at[t, rows(r)], lfin.at[t, rows(r)], flin_send.at[d, e], flin_recv.at[d, e], (s, row_at(d), tens(e))
         )
 
-    for d, e in others:
-        rsq(d, e).start()
-    for d, e in others:
-        rsq(d, e).wait_recv()
-    total = q_ref[rows(r), cols(t)]
-    for d, e in others:
-        total += rs_q[d, e]
-    red_q[...] = total
-
-    def l_fin(q):
-        return remote(red_q, lfin.at[rows(r), cols(t)], lf_send.at[q], lf_recv.at[0], (lax.rem(s + q, S), r, t))
-
     @pl.when(s < S - 1)
     def _():
-        for d, e in pairs:
-            l_hop(d, e).start()
+        for d in range(R):
+            l_hop(d).start()
+        gout[parts(r), :] = red_p[...]
+        for d in range(1, R):
+            fan(gout, fout_send, fout_recv, d).start()
+        g_fin(0).wait_recv()
+        for d in range(1, R):
+            fan_fin(d).start()
+        l_fin(0).wait_recv()
 
     @pl.when(s == S - 1)
     def _():
-        lfin[rows(r), cols(t)] = red_q[...]
+        lfin[t, rows(r)] = red_q[...]
         for q in range(1, S):
             l_fin(q).start()
 
-    def fan(buf, send, recv, d):
-        return remote(buf.at[rows(r)], buf.at[rows(r)], send.at[d], recv.at[d], (s, row_at(d), t))
-
-    def fan_l(d, e):
-        return remote(
-            lfin.at[rows(r), cols(t)], lfin.at[rows(r), cols(t)], flin_send.at[d, e], flin_recv.at[d, e],
-            (s, row_at(d), tens(e)),
-        )
-
-    for d in range(1, R):
-        fan(gout, fout_send, fout_recv, d).start()
-
-    @pl.when(s < S - 1)
-    def _():
-        g_fin(0).wait_recv()
-
-    for d in range(1, R):
-        fan(gfin, ffin_send, ffin_recv, d).start()
-
-    @pl.when(s < S - 1)
-    def _():
-        l_fin(0).wait_recv()
-
     for d, e in others:
         fan_l(d, e).start()
 
     for d in range(1, R):
-        fan(gout, fout_send, fout_recv, d).wait_recv()
-        fan(gfin, ffin_send, ffin_recv, d).wait_recv()
+        fan_fin(d).wait_recv()
+    final = unpack(gfin[...])
+    grams_out[2] = final
+
+    @pl.when(s == 0)
+    def _():
+        row = lax.broadcasted_iota(jnp.int32, (n, n), 0)
+        col = lax.broadcasted_iota(jnp.int32, (n, n), 1)
+        grams_out[0] = (row == col).astype(F32)
+
+    @pl.when(s > 0)
+    def _():
+        grams_out[0] = unpack(gin[...])
+
+    @pl.when(s < S - 1)
+    def _():
+        for d in range(1, R):
+            fan(gout, fout_send, fout_recv, d).wait_recv()
+        grams_out[1] = unpack(gout[...])
+
+    @pl.when(s == S - 1)
+    def _():
+        grams_out[1] = final
+
     for d, e in others:
         fan_l(d, e).wait_recv()
-    gin_out[...] = gin[...]
-    gout_out[...] = gout[...]
-    gfin_out[...] = gfin[...]
-    lfin_out[...] = lfin[...]
+    link = jnp.concatenate([lfin[0], lfin[1]], axis=1)
+
+    @pl.when(t == 0)
+    def _():
+        turned[...] = link
+
+    @pl.when(t == 1)
+    def _():
+        turned[...] = link.T
+
+    share = n // S
+    link_out[...] = turned[pl.ds(pl.multiple_of(s * share, share), share), :]
+    swap.wait_send()
     for d in range(1, R):
         rsp(d).wait_send()
-        fan(gout, fout_send, fout_recv, d).wait_send()
-        fan(gfin, ffin_send, ffin_recv, d).wait_send()
+        fan_fin(d).wait_send()
+        rsq(d).wait_send()
     for d, e in others:
-        rsq(d, e).wait_send()
         fan_l(d, e).wait_send()
+
+    @pl.when(s > 0)
+    def _():
+        l_half().wait_send()
 
     @pl.when(s < S - 1)
     def _():
         for d in range(R):
             g_hop(d).wait_send()
-        for d, e in pairs:
-            l_hop(d, e).wait_send()
+            l_hop(d).wait_send()
+        for d in range(1, R):
+            fan(gout, fout_send, fout_recv, d).wait_send()
 
     @pl.when(s == S - 1)
     def _():
@@ -332,30 +398,34 @@
 def chain(block, incoming, S, R):
     modes, n, _ = block.shape
     half = modes // 2
+    wide = n // 2
     group = 1
     while group < 4 and half % (2 * group) == 0:
         group *= 2
+    blocks = 3 if (3 * wide) % (8 * R) == 0 else 4
+    part = blocks * wide // R
     ch = n // R
     dma = pltpu.SemaphoreType.DMA
     vmem = pltpu.VMEM
-    full = jax.ShapeDtypeStruct((n, n), F32)
+    packed = vmem((blocks * wide, wide), F32)
+    halves = vmem((2, n, wide), F32)
     return pl.pallas_call(
-        functools.partial(chain_kernel, S, R, group),
-        out_shape=[full] * 4,
+        functools.partial(chain_kernel, S, R, group, blocks),
+        out_shape=[jax.ShapeDtypeStruct((3, n, n), F32), jax.ShapeDtypeStruct((n // S, n), F32)],
         in_specs=[pl.BlockSpec(memory_space=pl.ANY), pl.BlockSpec(memory_space=pltpu.VMEM)],
-        out_specs=[pl.BlockSpec(memory_space=pltpu.VMEM)] * 4,
+        out_specs=[pl.BlockSpec(memory_space=pltpu.VMEM)] * 2,
         scratch_shapes=[
             vmem((modes, n, n), F32), vmem((half, n, n), F32), vmem((n, n), F32),
             vmem((modes, n, n), BF16), vmem((modes, n, n), BF16),
             vmem((modes, n, n), BF16), vmem((modes, n, n), BF16),
             vmem((half, n, n), BF16), vmem((half, n, n), BF16),
-            vmem((n, n), F32), vmem((n, n), F32), vmem((n, n), F32), vmem((n, n), F32), vmem((n, n), F32),
-            vmem((n, n), F32), vmem((n, n), F32),
-            vmem((R, ch, n), F32), vmem((R, 2, ch, n // 2), F32),
-            vmem((ch, n), F32), vmem((ch, n // 2), F32), vmem((n, n), F32),
+            packed, packed, packed, halves, halves, packed, halves,
+            vmem((n, wide), F32), vmem((n, wide), F32),
+            vmem((R, part, wide), F32), vmem((R, ch, wide), F32),
+            vmem((part, wide), F32), vmem((ch, wide), F32), vmem((n, n), F32), vmem((n, n), F32),
             dma((modes // group,)), dma((2,)), dma((2,)),
-            dma((R,)), dma((R,)), dma((R, 2)), dma((R, 2)),
-            dma((R,)), dma((R,)), dma((R, 2)), dma((R, 2)),
+            dma((R,)), dma((R,)), dma((R,)), dma((R,)), dma, dma, dma, dma,
+            dma((R,)), dma((R,)), dma((R,)), dma((R,)),
             dma((R,)), dma((R,)), dma((R,)), dma((R,)), dma((R, 2)), dma((R, 2)),
             dma((S,)), dma((1,)), dma((S,)), dma((1,)),
         ],
@@ -378,7 +448,6 @@
     n = incoming_ref.shape[0]
     count = g_ref.shape[0]
     section = lax.axis_index("cores")
-    sections = lax.axis_size("cores")
 
     @pl.when(pl.program_id(0) == 0)
     def _():
@@ -393,20 +462,26 @@
             x = x_ref[m]
             return x, mm_nt(mm(x, g_ref[m]), x) - eye
 
-        def step(k, carry):
+        def step(carry):
+            k, _ = carry
+            distances = []
             for m in range(count):
                 x, e = residual(m)
                 x_ref[m] = x - mm(lower_part(e), x)
-            return carry
-
-        lax.fori_loop(0, NEWTON_STEPS, step, 0)
+                distances.append(jnp.sum(e * e))
+            return k + 1, tuple(distances)
+
+        def away(carry):
+            k, distances = carry
+            close = functools.reduce(jnp.logical_and, [d < CLOSE for d in distances])
+            return (k < NEWTON_STEPS) & jnp.logical_not(close)
+
+        _, distances = lax.while_loop(away, step, (0, (jnp.float32(1.0),) * count))
 
         for m in range(count):
-            x, e = residual(m)
-            distance = jnp.sum(e * e)
-            smallest = jnp.min(jnp.where(row == col, x, 1.0))
-
-            @pl.when(jnp.logical_not((distance < 1e-6) & (smallest > 0.0)))
+            smallest = jnp.min(jnp.where(row == col, x_ref[m], 1.0))
+
+            @pl.when(jnp.logical_not((distances[m] < CLOSE) & (smallest > 0.0)))
             def _(m=m):
                 a_ref[...] = g_ref[m]
                 b_ref[...] = eye
@@ -431,7 +506,9 @@
         def factor(m):
             return jnp.where(row <= col, mm(x_ref[m], g_ref[m]), 0.0)
 
-        tail_ref[...] = factor(2)
+        x_ref[2] = factor(2)
+        share = tail_ref.shape[0]
+        tail_ref[...] = x_ref[2, pl.ds(pl.multiple_of(section * share, share), share), :]
         upper = jnp.where(section == 0, incoming_ref[...], factor(0))
         hi, lo = split(upper)
         u_hi[...] = hi
@@ -442,19 +519,19 @@
 
     u3 = left3(u_hi[...], u_lo[...])
     x3 = right3(x_hi[...], x_lo[...])
+    mixed = dot(u3, jnp.concatenate([right3(*split(blocks_ref[j])) for j in range(group)], axis=1))
     for j in range(group):
-        mixed = dot(u3, right3(*split(blocks_ref[j])))
-        frames_ref[j] = dot(left3(*split(mixed)), x3)
-
-
-def make_frames(grams, incoming, block, scale):
+        frames_ref[j] = dot(left3(*split(mixed[:, j * n : (j + 1) * n])), x3)
+
+
+def make_frames(grams, incoming, block, scale, S):
     modes, n, _ = block.shape
     group = min(4, modes)
     vmem = pltpu.VMEM
     return pl.pallas_call(
         functools.partial(frame_kernel, group, scale),
         grid=(modes // group,),
-        out_shape=[jax.ShapeDtypeStruct((modes, n, n), F32), jax.ShapeDtypeStruct((n, n), F32)],
+        out_shape=[jax.ShapeDtypeStruct((modes, n, n), F32), jax.ShapeDtypeStruct((n // S, n), F32)],
         in_specs=[
             pl.BlockSpec((3, n, n), lambda i: (0, 0, 0)),
             pl.BlockSpec((n, n), lambda i: (0, 0)),
@@ -462,7 +539,7 @@
         ],
         out_specs=[
             pl.BlockSpec((group, n, n), lambda i: (i, 0, 0)),
-            pl.BlockSpec((n, n), lambda i: (0, 0)),
+            pl.BlockSpec((n // S, n), lambda i: (0, 0)),
         ],
         scratch_shapes=[
             vmem((3, n, n), F32), vmem((n, n), F32), vmem((n, n), F32),
@@ -477,17 +554,9 @@
     block = cores[0, 0]
     upper_start = incoming[0]
     n = block.shape[-1]
-    section = lax.axis_index("cores")
-    tensor = lax.axis_index("tensor")
-    gin, gout, gfin, link = chain(block, upper_start, S, R)
-    gin = jnp.where(section == 0, jnp.eye(n, dtype=F32), gin)
-    gout = jnp.where(section == S - 1, gfin, gout)
+    grams, link_rows = chain(block, upper_start, S, R)
     scale = float(modes_all * n) ** 0.5
-    frames, tail = make_frames(jnp.stack([gin, gout, gfin]), upper_start, block, scale)
-    share = n // S
-    link = jnp.where(tensor == 0, link, link.T)
-    tail_rows = lax.dynamic_slice_in_dim(tail, section * share, share, 0)
-    link_rows = lax.dynamic_slice_in_dim(link, section * share, share, 0)
+    frames, tail_rows = make_frames(grams, upper_start, block, scale, S)
     return frames[None, None], tail_rows[None], link_rows[None]
 
 

time: 172 us -> 146 us (0.85)
  the two profiles are of different devices: /device:TPU:31 before, /device:TPU:1 now
where the time goes in v2:
time: 146 us
  Pallas kernels  143 us (98%)
  local copies, waits for them, and re-layouts  1.76 us (1%)
    pallas_call x1, Pallas kernels, chain(): pl.pallas_call(functools.partial(chain_kernel, S, R, group, blocks), out_...  122 us
    pallas_call x1, Pallas kernels, make_frames(): pl.pallas_call(functools.partial(frame_kernel, group, scale), grid=(modes...  20.9 us

profile of v2, /device:TPU:1, one launch (start us, length us, event | category | flops | bytes accessed | tf_op | source)
XLA Modules:
  0.0 145.7 jit_solution(4962731194757401356)
XLA Ops:
  0.6 0.0 copy-start
  0.6 122.4 %gram_chain.1 = (f32[3,256,256]{2,1,0:T(8,128)}, f32[64,256]{1,0:T(8,128)}) custom-call(f32[32,256,256]{2,1,0:T(8,128)} %bitcast.7, f32[256,256]{1,0:T(8,128)} %bitcast.5), custom_call_target="tpu_custom_call" | custom-call | tf_op jit(solution)/shard_map/gram_chain/pallas_call | solution.py:412
  123.1 0.0 copy-done
  123.1 0.0 copy-start.1
  123.1 1.1 copy-done.1
  124.2 0.0 copy-start.2
  124.2 20.9 %frames.1 = (f32[32,256,256]{2,1,0:T(8,128)}, f32[64,256]{1,0:T(8,128)}) custom-call(f32[3,256,256]{2,1,0:T(8,128)S(1)} %copy-done.1, f32[256,256]{1,0:T(8,128)S(1)} %bitcast.6, f32[32,256,256]{2,1,0:T(8,128)} %bitcast.8), custom_call_target="tpu_custom_call" | custom-call | tf_op jit(solution)/shard_map/frames/pallas_call | solution.py:531
  145.1 0.0 copy-done.2
  145.1 0.6 copy.6
Async XLA Ops:
  0.6 122.4 %copy-start = (f32[1,256,256]{2,1,0:T(8,128)S(1)}, f32[1,256,256]{2,1,0:T(8,128)}, u32[]{:S(2)}) copy-start(f32[1,256,256]{2,1,0:T(8,128)} %param.3) | copy-start | bytes 786436
  123.1 1.1 copy-start.1
  124.2 20.9 %copy-start.2 = (f32[64,256]{1,0:T(8,128)S(1)}, f32[64,256]{1,0:T(8,128)}, u32[]{:S(2)}) copy-start(f32[64,256]{1,0:T(8,128)} %get-tuple-element.10) | copy-start | bytes 196612

commit v3 on v2

--- a/solution.py
+++ b/solution.py
@@ -12,6 +12,7 @@
 BF16 = jnp.bfloat16
 NEWTON_STEPS = 16
 CLOSE = 1e-6
+WARM_STEPS = 2
 
 
 def split(x):
@@ -63,10 +64,27 @@
     )
 
 
+def lower_part(e):
+    row = lax.broadcasted_iota(jnp.int32, e.shape, 0)
+    col = lax.broadcasted_iota(jnp.int32, e.shape, 1)
+    return jnp.where(row > col, e, jnp.where(row == col, 0.5 * e, 0.0))
+
+
+def first_guess(g, eye):
+    dr = lax.rsqrt(jnp.sum(g * eye, axis=0, keepdims=True))
+    dc = lax.rsqrt(jnp.sum(g * eye, axis=1, keepdims=True))
+    return (eye - lower_part(g * dr * dc - eye)) * dr
+
+
+def newton(x, g, eye):
+    e = mm_nt(mm(x, g), x) - eye
+    return x - mm(lower_part(e), x), e
+
+
 def chain_kernel(
     S, R, group, blocks,
     cores_ref, incoming_ref,
-    grams_out, link_out,
+    grams_out, x_out, link_out,
     raw, other, in_other, c_hi, c_lo, ct_hi, ct_lo, o_hi, o_lo,
     gin, gout, gfin, lin, lfin, p_ref, q_ref, q_got, q_sum, rs_p, rs_q, red_p, red_q, acc, turned,
     raw_sem, pair_send, pair_recv,
@@ -334,11 +352,13 @@
     final = unpack(gfin[...])
     grams_out[2] = final
 
+    row = lax.broadcasted_iota(jnp.int32, (n, n), 0)
+    col = lax.broadcasted_iota(jnp.int32, (n, n), 1)
+    eye = (row == col).astype(F32)
+
     @pl.when(s == 0)
     def _():
-        row = lax.broadcasted_iota(jnp.int32, (n, n), 0)
-        col = lax.broadcasted_iota(jnp.int32, (n, n), 1)
-        grams_out[0] = (row == col).astype(F32)
+        grams_out[0] = eye
 
     @pl.when(s > 0)
     def _():
@@ -353,6 +373,17 @@
     @pl.when(s == S - 1)
     def _():
         grams_out[1] = final
+
+    for m in range(3):
+        x_out[m] = first_guess(grams_out[m], eye)
+
+    def warm(k, carry):
+        new = [newton(x_out[m], grams_out[m], eye)[0] for m in range(3)]
+        for m in range(3):
+            x_out[m] = new[m]
+        return carry
+
+    lax.fori_loop(0, WARM_STEPS, warm, 0)
 
     for d, e in others:
         fan_l(d, e).wait_recv()
@@ -411,9 +442,9 @@
     halves = vmem((2, n, wide), F32)
     return pl.pallas_call(
         functools.partial(chain_kernel, S, R, group, blocks),
-        out_shape=[jax.ShapeDtypeStruct((3, n, n), F32), jax.ShapeDtypeStruct((n // S, n), F32)],
+        out_shape=[jax.ShapeDtypeStruct((3, n, n), F32)] * 2 + [jax.ShapeDtypeStruct((n // S, n), F32)],
         in_specs=[pl.BlockSpec(memory_space=pl.ANY), pl.BlockSpec(memory_space=pltpu.VMEM)],
-        out_specs=[pl.BlockSpec(memory_space=pltpu.VMEM)] * 2,
+        out_specs=[pl.BlockSpec(memory_space=pltpu.VMEM)] * 3,
         scratch_shapes=[
             vmem((modes, n, n), F32), vmem((half, n, n), F32), vmem((n, n), F32),
             vmem((modes, n, n), BF16), vmem((modes, n, n), BF16),
@@ -436,14 +467,8 @@
     )(block, incoming)
 
 
-def lower_part(e):
-    row = lax.broadcasted_iota(jnp.int32, e.shape, 0)
-    col = lax.broadcasted_iota(jnp.int32, e.shape, 1)
-    return jnp.where(row > col, e, jnp.where(row == col, 0.5 * e, 0.0))
-
-
 def frame_kernel(
-    group, scale, g_ref, incoming_ref, blocks_ref, frames_ref, tail_ref, x_ref, a_ref, b_ref, u_hi, u_lo, x_hi, x_lo
+    group, scale, g_ref, start_ref, incoming_ref, blocks_ref, frames_ref, tail_ref, x_ref, a_ref, b_ref, u_hi, u_lo, x_hi, x_lo
 ):
     n = incoming_ref.shape[0]
     count = g_ref.shape[0]
@@ -454,20 +479,14 @@
         row = lax.broadcasted_iota(jnp.int32, (n, n), 0)
         col = lax.broadcasted_iota(jnp.int32, (n, n), 1)
         eye = (row == col).astype(F32)
-        for m in range(count):
-            diagonal = jnp.sum(g_ref[m] * eye, axis=0, keepdims=True)
-            x_ref[m] = eye * lax.rsqrt(diagonal)
-
-        def residual(m):
-            x = x_ref[m]
-            return x, mm_nt(mm(x, g_ref[m]), x) - eye
+        x_ref[...] = start_ref[...]
 
         def step(carry):
             k, _ = carry
+            new = [newton(x_ref[m], g_ref[m], eye) for m in range(count)]
             distances = []
-            for m in range(count):
-                x, e = residual(m)
-                x_ref[m] = x - mm(lower_part(e), x)
+            for m, (x, e) in enumerate(new):
+                x_ref[m] = x
                 distances.append(jnp.sum(e * e))
             return k + 1, tuple(distances)
 
@@ -524,7 +543,7 @@
         frames_ref[j] = dot(left3(*split(mixed[:, j * n : (j + 1) * n])), x3)
 
 
-def make_frames(grams, incoming, block, scale, S):
+def make_frames(grams, start, incoming, block, scale, S):
     modes, n, _ = block.shape
     group = min(4, modes)
     vmem = pltpu.VMEM
@@ -533,6 +552,7 @@
         grid=(modes // group,),
         out_shape=[jax.ShapeDtypeStruct((modes, n, n), F32), jax.ShapeDtypeStruct((n // S, n), F32)],
         in_specs=[
+            pl.BlockSpec((3, n, n), lambda i: (0, 0, 0)),
             pl.BlockSpec((3, n, n), lambda i: (0, 0, 0)),
             pl.BlockSpec((n, n), lambda i: (0, 0)),
             pl.BlockSpec((group, n, n), lambda i: (i, 0, 0)),
@@ -547,16 +567,16 @@
         ],
         compiler_params=pltpu.CompilerParams(vmem_limit_bytes=48 * 1024 * 1024),
         name="frames",
-    )(grams, incoming, block)
+    )(grams, start, incoming, block)
 
 
 def shards(S, R, T, modes_all, cores, incoming):
     block = cores[0, 0]
     upper_start = incoming[0]
     n = block.shape[-1]
-    grams, link_rows = chain(block, upper_start, S, R)
+    grams, start, link_rows = chain(block, upper_start, S, R)
     scale = float(modes_all * n) ** 0.5
-    frames, tail_rows = make_frames(grams, upper_start, block, scale, S)
+    frames, tail_rows = make_frames(grams, start, upper_start, block, scale, S)
     return frames[None, None], tail_rows[None], link_rows[None]
 
 

time: 146 us -> 142 us (0.973)
  Pallas kernels: 143 us -> 138 us
    pallas_call x1, Pallas kernels: 20.9 us -> 15.1 us  [make_frames(): pl.pallas_call(functools.partial(frame_kernel, group, scale), grid=(modes...]
where the time goes in v3:
time: 142 us; the launch traced here: 141 us
  Pallas kernels  138 us (97%)
  local copies, waits for them, and re-layouts  2.9 us (2%)
    pallas_call x1, Pallas kernels, chain(): pl.pallas_call(functools.partial(chain_kernel, S, R, group, blocks), out_...  123 us
    pallas_call x1, Pallas kernels, make_frames(): pl.pallas_call(functools.partial(frame_kernel, group, scale), grid=(modes...  15.1 us
    unnamed x9, local copies, waits for them, and re-layouts  2.9 us

profile of v3, /device:TPU:1, one launch (start us, length us, event | category | flops | bytes accessed | tf_op | source)
XLA Modules:
  0.0 141.4 jit_solution(16906732854521558551)
XLA Ops:
  0.6 0.0 copy-start
  0.6 122.7 %gram_chain.1 = (f32[3,256,256]{2,1,0:T(8,128)}, f32[3,256,256]{2,1,0:T(8,128)}, f32[64,256]{1,0:T(8,128)}) custom-call(f32[32,256,256]{2,1,0:T(8,128)} %bitcast.7, f32[256,256]{1,0:T(8,128)} %bitcast.5), custom_call_target="tpu_custom_call" | custom-call | tf_op jit(solution)/shard_map/gram_chain/pallas_call | solution.py:443
  123.3 0.0 copy-done
  123.4 0.0 copy-start.1
  123.4 1.1 copy-done.1
  124.5 0.0 copy-start.2
  124.5 1.1 copy-done.2
  125.6 0.0 copy-start.3
  125.6 15.1 %frames.1 = (f32[32,256,256]{2,1,0:T(8,128)}, f32[64,256]{1,0:T(8,128)}) custom-call(f32[3,256,256]{2,1,0:T(8,128)S(1)} %copy-done.1, f32[3,256,256]{2,1,0:T(8,128)S(1)} %copy-done.2, f32[256,256]{1,0:T(8,128)S(1)} %bitcast.6, f32[32,256,256]{2,1,0:T(8,128)} %bitcast.8), custom_call_target="tpu_custom_call" | custom-call | tf_op jit(solution)/shard_map/frames/pallas_call | solution.py:550
  140.8 0.0 copy-done.3
  140.8 0.6 copy.6
Async XLA Ops:
  0.6 122.7 %copy-start = (f32[1,256,256]{2,1,0:T(8,128)S(1)}, f32[1,256,256]{2,1,0:T(8,128)}, u32[]{:S(2)}) copy-start(f32[1,256,256]{2,1,0:T(8,128)} %param.3) | copy-start | bytes 786436
  123.4 1.1 copy-start.1
  124.5 1.1 copy-start.2
  125.6 15.1 %copy-start.3 = (f32[64,256]{1,0:T(8,128)S(1)}, f32[64,256]{1,0:T(8,128)}, u32[]{:S(2)}) copy-start(f32[64,256]{1,0:T(8,128)} %get-tuple-element.12) | copy-start | bytes 196612
